TPU v7x, 512 devices: a whole 4x4x16 slice. The times are simulated.
512 devices in a mesh: node: 64 (over y, z), local: 8 (over x, core).
Axes of the slice: x: 4, y: 4, z: 16, core: 2. Of those that a mesh axis runs over, the one named last changes fastest.
Arguments:
- grad_out: bfloat16 [65536, 3584], P(('node', 'local')), may hold values from -6 to 6
- expert_ids: int32 [65536, 8], P(('node', 'local')), may hold values from 0 to 255, as said below
- gate_weights: float32 [65536, 8], P(('node', 'local')), may hold values from 0.05 to 0.35
- saved_hidden: bfloat16 [64, 1024, 1024], P('node', None, 'local'), may hold values from -0.59765625 to 0.59765625
- down_weight: bfloat16 [64, 1024, 3584], P('node', 'local'), may hold values from -0.1875 to 0.1875
- second_moment: bfloat16 [64, 1024, 3584], P('node', 'local'), may hold values from 0.0019989014 to 0.25
Outputs:
- gate_weight_gradient: float32 [65536, 8], P(('node', 'local'))
- hidden_grad: bfloat16 [64, 1024, 1024], P('node', None, 'local')
- new_weight: bfloat16 [64, 1024, 3584], P('node', 'local')
- new_second: bfloat16 [64, 1024, 3584], P('node', 'local')
Inputs may be any that keep to these rules, and one draw needn't show every extreme that they name: `expert_ids`: each row names 8 different experts on at most 4 nodes (node = id // 4), two on each; at most one per row is in flight (id % 4 == 0). Among the rows of one device at most 2 name the in-flight expert of any one node, and in every draw some node receives exactly 2 from every device.
All inputs are finite; a program needn't handle non-finite values.
Results may differ from a plain program's by a relative error of at most 0.0051.
Values may be sent and summed in bfloat16 or wider, within the bound.
No kernel may reach another device: no remote copies, remote signals or barrier semaphores. Data moves between devices by JAX's collectives and lax.ppermute only.
A program may use at most 128 MiB of HBM per device.

v0:
```python
import jax
import jax.numpy as jnp
from jax import lax
from jax.sharding import PartitionSpec as P

EXPERTS_PER_HOST = 4
CAP = 2
beta_second = 0.95
learn_rate = 0.002
decay_rate = 0.1
epsilon = 1e-08
correct_second = 0.994079470779666


def gather_rows(picked_experts, gate_values, grads, node_count):
    transit_rows = picked_experts % EXPERTS_PER_HOST == 0
    row_present = jnp.any(transit_rows, 1)
    destination_node = jnp.sum(jnp.where(transit_rows, picked_experts // EXPERTS_PER_HOST, 0), 1)
    onehot = (
        (destination_node[:, None] == jnp.arange(node_count, dtype=jnp.int32)[None, :])
        & row_present[:, None]
    ).astype(jnp.int32)
    within_rank = jnp.sum(onehot * (jnp.cumsum(onehot, 0) - 1), 1)
    slot_index = destination_node * CAP + within_rank
    expert_location = (
        jnp.arange(node_count * CAP, dtype=jnp.int32)[:, None] == slot_index[None, :]
    ) & row_present[None, :]
    matched_gate = jnp.sum(jnp.where(transit_rows, gate_values, 0.0), 1).astype(jnp.bfloat16)
    departing_rows = jnp.dot(
        expert_location.astype(jnp.bfloat16), grads, preferred_element_type=jnp.float32
    ).astype(jnp.bfloat16)
    departing_gates = jnp.sum(
        jnp.where(expert_location, matched_gate.astype(jnp.float32)[None, :], 0.0), 1
    ).astype(jnp.bfloat16)
    feature_count = grads.shape[1]
    return (
        departing_rows.reshape(node_count, CAP, feature_count),
        departing_gates.reshape(node_count, CAP),
        expert_location,
        transit_rows,
    )


def on_device(grad_out, expert_ids, gate_weights, saved_hidden, down_weight, second_moment):
    node_count = lax.axis_size("node")
    members = lax.axis_size("local")
    feature_count = grad_out.shape[1]
    departing_rows, departing_gates, expert_location, transit_rows = gather_rows(
        expert_ids, gate_weights, grad_out, node_count
    )
    copies, copy_gates = (
        lax.all_gather(departing_rows[None], "local", axis=0, tiled=True),
        lax.all_gather(departing_gates[None], "local", axis=0, tiled=True),
    )
    arrived, arrived_gates = (
        lax.all_to_all(copies, "node", split_axis=1, concat_axis=1, tiled=True),
        lax.all_to_all(copy_gates, "node", split_axis=1, concat_axis=1, tiled=True),
    )
    arrived_rows = arrived.reshape(-1, feature_count)
    slot_gates = arrived_gates.reshape(-1).astype(jnp.float32)
    weight_now = down_weight[0]
    hidden_now = saved_hidden[0]
    unscaled = lax.dot_general(
        arrived_rows, weight_now, (((1,), (1,)), ((), ())), preferred_element_type=jnp.float32
    )
    hidden_out = (slot_gates[:, None] * unscaled).astype(jnp.bfloat16)
    slot_score = jnp.sum(unscaled * hidden_now.astype(jnp.float32), 1)
    scaled = (slot_gates[:, None] * arrived_rows.astype(jnp.float32)).astype(jnp.bfloat16)
    grad = lax.dot_general(
        hidden_now, scaled, (((0,), (0,)), ((), ())), preferred_element_type=jnp.float32
    )
    second_new = (
        beta_second * second_moment[0].astype(jnp.float32) + (1.0 - beta_second) * grad * grad
    )
    weight_f = weight_now.astype(jnp.float32)
    update = grad / (jnp.sqrt(second_new / correct_second) + epsilon) + decay_rate * weight_f
    weight_new = weight_f - learn_rate * update
    score_terms = slot_score.reshape(members, node_count * CAP)
    summed = lax.psum(score_terms, "local")
    own_terms = lax.dynamic_slice_in_dim(summed, lax.axis_index("local"), 1, 0)
    returned = lax.all_to_all(
        own_terms.reshape(node_count, CAP), "node", split_axis=0, concat_axis=0, tiled=True
    )
    returned_flat = returned.reshape(node_count * CAP)
    token_gradient = jnp.sum(jnp.where(expert_location, returned_flat[:, None], 0.0), 0)
    gate_weight_gradient = jnp.where(transit_rows, token_gradient[:, None], 0.0)
    return (
        gate_weight_gradient,
        hidden_out[None],
        weight_new.astype(jnp.bfloat16)[None],
        second_new.astype(jnp.bfloat16)[None],
    )


def solution(mesh):
    return jax.shard_map(
        on_device,
        mesh=mesh,
        in_specs=(
            P(("node", "local"), None),
            P(("node", "local"), None),
            P(("node", "local"), None),
            P("node", None, "local"),
            P("node", "local", None),
            P("node", "local", None),
        ),
        out_specs=(
            P(("node", "local"), None),
            P("node", None, "local"),
            P("node", "local", None),
            P("node", "local", None),
        ),
        check_vma=False,
    )
```

profile of v0, /device:TPU:2, one launch (start us, length us, event | category | flops | bytes accessed | tf_op | source)
XLA Modules:
  0.0 566.0 jit_solution(3273625820910826075)
XLA Ops:
  7.2 0.0 copy-start
  7.2 0.0 all-gather.2.cloned.1.call-start
  7.2 0.8 fusion.22
  8.0 0.7 fusion.19
  8.7 0.1 fusion.14
  8.8 0.2 reduce_window_sum.11
  9.0 0.2 select_reduce_fusion.2
  9.2 0.0 copy-done
  9.2 0.4 convolution_convert_fusion
  9.6 0.3 broadcast_in_dim_reshape.2
  9.9 1.0 copy.65
  11.0 0.0 all-gather.2.cloned.1.call-update
  11.0 56.7 %all-gather.2.cloned.1.call-done = bf16[8,64,2,3584]{3,1,2,0:T(8,128)(2,1)} async-done(((bf16[1,64,2,3584]{3,1,2,0:T(8,128)(2,1)}), bf16[8,64,2,3584]{3,1,2,0:T(8,128)(2,1)}) %all-gather.2.cloned.1.call-update) | async-done | bytes 7340048 | tf_op jit(solution)/shard_map/all_gather | solution.py:52
  67.7 14.7 %copy.66 = bf16[8,64,2,3584]{3,2,0,1:T(2,128)(2,1)} copy(bf16[8,64,2,3584]{3,1,2,0:T(8,128)(2,1)} %all-gather.2.cloned.1.call-done) | data formatting | bytes 14680064 | tf_op jit(solution)/shard_map/all_gather | solution.py:52
  82.4 0.0 copy-start.5
  82.4 16.0 %all-to-all-start = ((bf16[8,64,2,3584]{3,2,0,1:T(2,128)(2,1)}), bf16[8,64,2,3584]{3,2,0,1:T(2,128)(2,1)}, u32[]{:S(2)}, u32[]{:S(2)}) async-start(bf16[8,64,2,3584]{3,2,0,1:T(2,128)(2,1)} %copy.66), calls=%async_computation | async-start | bytes 14680064 | tf_op jit(solution)/shard_map/all_to_all | solution.py:56
  98.4 0.0 copy-done.5
  98.4 0.1 copy.69
  98.6 323.8 %all-to-all-done = bf16[8,64,2,3584]{3,2,0,1:T(2,128)(2,1)} async-done(((bf16[8,64,2,3584]{3,2,0,1:T(2,128)(2,1)}), bf16[8,64,2,3584]{3,2,0,1:T(2,128)(2,1)}, u32[]{:S(2)}, u32[]{:S(2)}) %all-to-all-start) | async-done | bytes 7340064 | tf_op jit(solution)/shard_map/all_to_all | solution.py:56
  422.4 7.4 %copy.67 = bf16[8,64,2,3584]{3,2,1,0:T(2,128)(2,1)} copy(bf16[8,64,2,3584]{3,2,0,1:T(2,128)(2,1)} %all-to-all-done) | data formatting | bytes 14680064 | tf_op jit(solution)/shard_map/all_to_all | solution.py:56
  429.8 0.0 copy-start.2
  429.8 15.5 %reshape.62 = bf16[1024,3584]{1,0:T(8,128)(2,1)} reshape(bf16[8,64,2,3584]{3,2,1,0:T(2,128)(2,1)} %copy.67) | data formatting | bytes 14680064 | tf_op jit(solution)/shard_map/reshape | solution.py:59
  445.4 0.0 copy-done.2
  445.4 0.0 copy-start.6
  445.4 5.6 multiply_reduce_fusion
  450.9 0.0 copy-start.3
  451.0 10.5 %psum.7 = f32[8,128]{1,0:T(8,128)S(1)} all-reduce(f32[8,128]{1,0:T(8,128)S(1)} %bitcast.41), channel_id=1, replica_groups=mesh['node'=64,'local'=8] {'local'}, use_global_device_ids=true, to_apply=%region_5.6 | all-reduce | flops 1024 | bytes 8192 | tf_op jit(solution)/shard_map/psum | solution.py:79
  461.5 0.8 all_to_all.13
  462.2 7.0 %all-to-all-start.1 = ((f32[64,1,2]{2,1,0:T(1,128)}), f32[64,1,2]{2,1,0:T(1,128)}, u32[]{:S(2)}, u32[]{:S(2)}) async-start(f32[64,1,2]{2,1,0:T(1,128)} %bitcast.3), calls=%async_computation.1 | async-start | bytes 65536 | tf_op jit(solution)/shard_map/all_to_all | solution.py:81
  469.2 0.0 copy-done.6
  469.2 0.5 select_reduce_fusion.3
  469.8 0.6 copy.68
  470.4 0.7 convert_element_type.132
  471.1 0.0 copy-done.3
  471.1 0.6 copy.78
  471.7 11.6 %all-to-all-done.1 = f32[64,1,2]{2,1,0:T(1,128)} async-done(((f32[64,1,2]{2,1,0:T(1,128)}), f32[64,1,2]{2,1,0:T(1,128)}, u32[]{:S(2)}, u32[]{:S(2)}) %all-to-all-start.1) | async-done | bytes 544 | tf_op jit(solution)/shard_map/all_to_all | solution.py:81
  483.3 0.5 broadcast.47
  483.8 1.5 reduce.7
  485.3 0.1 broadcast_in_dim.59
  485.4 0.1 select_reduce_fusion
  485.6 0.2 convert_element_type.82
  485.7 0.1 copy.71
  485.8 11.1 %all_gather.7 = bf16[8,64,2]{1,2,0:T(2,128)(2,1)S(1)} all-gather(bf16[1,64,2]{1,2,0:T(2,128)(2,1)S(1)} %copy.71), channel_id=1, replica_groups=mesh['node'=64,'local'=8] {'local'}, dimensions={0}, use_global_device_ids=true | all-gather | bytes 2304 | tf_op jit(solution)/shard_map/all_gather | solution.py:53
  496.9 0.7 copy.72
  497.6 4.8 all-to-all-start.2
  502.4 0.6 broadcast_select_fusion
  503.0 13.6 %all-to-all-done.2 = bf16[8,64,2]{0,2,1:T(2,128)(2,1)S(1)} async-done(((bf16[8,64,2]{0,2,1:T(2,128)(2,1)}), bf16[8,64,2]{0,2,1:T(2,128)(2,1)S(1)}, u32[]{:S(2)}, u32[]{:S(2)}) %all-to-all-start.2) | async-done | bytes 2080 | tf_op jit(solution)/shard_map/all_to_all | solution.py:57
  516.6 0.1 copy.73
  516.7 0.2 copy.74
  516.8 7.8 %multiply_convert_fusion = bf16[8,64,2,3584]{3,1,2,0:T(8,128)(2,1)S(1)} fusion(bf16[8,64,2,3584]{3,2,0,1:T(2,128)(2,1)} %all-to-all-done, f32[8,64,2]{1,2,0:T(2,128)S(1)} %copy.75), kind=kLoop, calls=%fused_computation | loop fusion | flops 11010048 | bytes 14684160 | tf_op jit(solution)/shard_map/convert_element_type | solution.py:68
  524.6 7.1 %copy.77 = bf16[8,64,2,3584]{3,2,1,0:T(2,128)(2,1)} copy(bf16[8,64,2,3584]{3,1,2,0:T(8,128)(2,1)S(1)} %multiply_convert_fusion) | data formatting | bytes 14680064 | tf_op jit(solution)/shard_map/convert_element_type | solution.py:68
  531.7 15.4 %convert_element_type.90 = bf16[1024,3584]{1,0:T(8,128)(2,1)} reshape(bf16[8,64,2,3584]{3,2,1,0:T(2,128)(2,1)} %copy.77) | data formatting | bytes 14680064 | tf_op jit(solution)/shard_map/convert_element_type | solution.py:68
  547.1 7.3 %fusion.5 = (bf16[1,128,3584]{1,2,0:T(8,128)(2,1)}, bf16[1,128,3584]{1,2,0:T(8,128)(2,1)}) fusion(bf16[1,128,3584]{1,2,0:T(8,128)(2,1)S(1)} %copy.78, bf16[1,128,3584]{1,2,0:T(8,128)(2,1)S(1)} %copy.68, bf16[1024,3584]{1,0:T(8,128)(2,1)} %convert_element_type.90, bf16[1,1024,128]{2,1,0:T(8,128)(2,1)S(1)} %copy-done.5), kind=kOutput, calls=%fused_computation.11 | convolution fusion | flops 946405376 | bytes 11272192 | tf_op jit(solution)/shard_map/dot_general | solution.py:69
  554.5 0.0 copy-start.4
  554.5 0.0 copy-start.1
  554.5 2.3 copy.80
  556.8 0.0 copy-done.4
  556.8 1.3 copy.81
  558.1 0.2 reshape.64
  558.3 0.8 copy.79
  559.1 0.0 copy-done.1
  (4 shorter events, 0.1 us)
Async XLA Ops:
  7.2 2.0 copy-start
  7.2 60.5 %all-gather.2.cloned.1.call-start = ((), (), s32[]{:S(2)}) async-start(), calls=%async_computation.3 | async-start | bytes 8257536 | tf_op jit(solution)/shard_map/all_gather | solution.py:52
  82.4 16.0 %copy-start.5 = (bf16[1,1024,128]{2,1,0:T(8,128)(2,1)S(1)}, bf16[1,1024,128]{2,1,0:T(8,128)(2,1)}, u32[]{:S(2)}) copy-start(bf16[1,1024,128]{2,1,0:T(8,128)(2,1)} %param.9) | copy-start | bytes 786436
  82.4 340.0 %all-to-all-start = ((bf16[8,64,2,3584]{3,2,0,1:T(2,128)(2,1)}), bf16[8,64,2,3584]{3,2,0,1:T(2,128)(2,1)}, u32[]{:S(2)}, u32[]{:S(2)}) async-start(bf16[8,64,2,3584]{3,2,0,1:T(2,128)(2,1)} %copy.66), calls=%async_computation | async-start | bytes 14680064 | tf_op jit(solution)/shard_map/all_to_all | solution.py:56
  429.8 15.5 %copy-start.2 = (bf16[1,128,3584]{2,1,0:T(8,128)(2,1)S(1)}, bf16[1,128,3584]{2,1,0:T(8,128)(2,1)}, u32[]{:S(2)}) copy-start(bf16[1,128,3584]{2,1,0:T(8,128)(2,1)} %param.10) | copy-start | bytes 2752516
  445.4 23.9 %copy-start.6 = (f32[128,8]{0,1:T(8,128)S(1)}, f32[128,8]{0,1:T(8,128)}, u32[]{:S(2)}) copy-start(f32[128,8]{0,1:T(8,128)} %param.8) | copy-start | bytes 12292
  450.9 20.1 %copy-start.3 = (bf16[1,128,3584]{2,1,0:T(8,128)(2,1)S(1)}, bf16[1,128,3584]{2,1,0:T(8,128)(2,1)}, u32[]{:S(2)}) copy-start(bf16[1,128,3584]{2,1,0:T(8,128)(2,1)} %param.11) | copy-start | bytes 2752516
  462.2 21.0 %all-to-all-start.1 = ((f32[64,1,2]{2,1,0:T(1,128)}), f32[64,1,2]{2,1,0:T(1,128)}, u32[]{:S(2)}, u32[]{:S(2)}) async-start(f32[64,1,2]{2,1,0:T(1,128)} %bitcast.3), calls=%async_computation.1 | async-start | bytes 65536 | tf_op jit(solution)/shard_map/all_to_all | solution.py:81
  497.6 19.0 %all-to-all-start.2 = ((bf16[8,64,2]{0,2,1:T(2,128)(2,1)}), bf16[8,64,2]{0,2,1:T(2,128)(2,1)S(1)}, u32[]{:S(2)}, u32[]{:S(2)}) async-start(bf16[8,64,2]{0,2,1:T(2,128)(2,1)} %copy.72), calls=%async_computation.2 | async-start | bytes 65536 | tf_op jit(solution)/shard_map/all_to_all | solution.py:57
  554.5 2.4 copy-start.4
  554.5 4.7 copy-start.1
Sparse Core Ops, SparseCore 0:
  11.1 56.5 all-gather.1
where the time goes:
time: 567 us; the launch traced here: 566 us
  waiting for transfers between devices  406 us (72%)
  local copies, waits for them, and re-layouts  70.1 us (12%)
  starting transfers between devices  27.8 us (5%)
  blocking collectives  21.6 us (4%)
  between operations  14.2 us (3%)
  matrix products  13.3 us (2%)
  other arithmetic  13.2 us (2%)
    all_to_all x1, waiting for transfers between devices, on_device(): lax.all_to_all(copies, 'node', split_axis=1, concat_axis=1, tiled=True)  324 us
    all_gather x1, waiting for transfers between devices, on_device(): lax.all_gather(departing_rows[None], 'local', axis=0, tiled=True)  56.7 us
    convert_element_type x2, local copies, waits for them, and re-layouts, on_device(): (slot_gates[:, None] * arrived_rows.astype(jnp.float32)).astype(jnp.bfloa...  22.5 us
    all_to_all x1, starting transfers between devices, on_device(): lax.all_to_all(copies, 'node', split_axis=1, concat_axis=1, tiled=True)  16 us
    reshape x1, local copies, waits for them, and re-layouts, on_device(): arrived_rows = arrived.reshape(-1, feature_count)  15.5 us
    all_gather x1, local copies, waits for them, and re-layouts, on_device(): lax.all_gather(departing_rows[None], 'local', axis=0, tiled=True)  14.7 us
    all_to_all x1, waiting for transfers between devices, on_device(): lax.all_to_all(copy_gates, 'node', split_axis=1, concat_axis=1, tiled=True)  13.6 us
    all_to_all x1, waiting for transfers between devices, on_device(): lax.all_to_all(own_terms.reshape(node_count, CAP), 'node', split_axis=0,...  11.6 us
  transfers between devices with their start and end apart: 4, of which 4 were waited for; matrix products, arithmetic and copies ran while one was open for 1% of the time, Pallas kernels for 0%

commit v1 on v0

--- a/solution.py
+++ b/solution.py
@@ -52,8 +52,14 @@
         lax.all_gather(departing_rows[None], "local", axis=0, tiled=True),
         lax.all_gather(departing_gates[None], "local", axis=0, tiled=True),
     )
+    files_extend = lambda m, mesh_ax: jnp.concatenate(
+        lax.all_to_all(
+            jnp.stack(jnp.split(m, lax.axis_size(mesh_ax), axis=1), axis=0), mesh_ax, 0, 0
+        ),
+        axis=1,
+    )
     arrived, arrived_gates = (
-        lax.all_to_all(copies, "node", split_axis=1, concat_axis=1, tiled=True),
+        files_extend(copies, "node"),
         lax.all_to_all(copy_gates, "node", split_axis=1, concat_axis=1, tiled=True),
     )
     arrived_rows = arrived.reshape(-1, feature_count)

time: 567 us -> 665 us (1.17)
  local copies, waits for them, and re-layouts: 70.1 us -> 167 us
    unnamed x20 -> x81, local copies, waits for them, and re-layouts: 5.85 us -> 110 us
    another operation x0 -> x2, local copies, waits for them, and re-layouts: none -> 17.2 us  [the longest x1 15.5 us: on_device(): arrived_rows = arrived.reshape(-1, feature_count)]
    all_gather x1 -> x0, local copies, waits for them, and re-layouts: 14.7 us -> none  [on_device(): lax.all_gather(departing_rows[None], 'local', axis=0, tiled=True)]
    reshape x1, local copies, waits for them, and re-layouts: 15.5 us -> 7.06 us  [on_device(): jnp.concatenate(lax.all_to_all(jnp.stack(jnp.split(m, lax.axis_size(mesh_...]
  transfers between devices with their start and end apart: 4 -> 4, of which waited for: 4 -> 4; matrix products, arithmetic and copies ran while one was open for 1% -> 0% of each run, Pallas kernels for 0% -> 0%
where the time goes in v1:
time: 665 us; the launch traced here: 663 us
  waiting for transfers between devices  406 us (61%)
  local copies, waits for them, and re-layouts  167 us (25%)
  starting transfers between devices  28 us (4%)
  blocking collectives  21.5 us (3%)
  between operations  14.2 us (2%)
  matrix products  13.6 us (2%)
  other arithmetic  12 us (2%)
    all_to_all x1, waiting for transfers between devices, on_device(): lax.all_to_all(jnp.stack(jnp.split(m, lax.axis_size(mesh_ax), axis=1), ax...  324 us
    unnamed x81, local copies, waits for them, and re-layouts  110 us
    all_gather x1, waiting for transfers between devices, on_device(): lax.all_gather(departing_rows[None], 'local', axis=0, tiled=True)  56.7 us
    convert_element_type x2, local copies, waits for them, and re-layouts, on_device(): (slot_gates[:, None] * arrived_rows.astype(jnp.float32)).astype(jnp.bfloa...  22.5 us
    all_to_all x1, starting transfers between devices, on_device(): lax.all_to_all(jnp.stack(jnp.split(m, lax.axis_size(mesh_ax), axis=1), ax...  16.2 us
    another operation x1, local copies, waits for them, and re-layouts, on_device(): arrived_rows = arrived.reshape(-1, feature_count)  15.5 us
    all_to_all x1, waiting for transfers between devices, on_device(): lax.all_to_all(copy_gates, 'node', split_axis=1, concat_axis=1, tiled=True)  13.6 us
  transfers between devices with their start and end apart: 4, of which 4 were waited for; matrix products, arithmetic and copies ran while one was open for 0% of the time, Pallas kernels for 0%

profile of v1, /device:TPU:2, one launch (start us, length us, event | category | flops | bytes accessed | tf_op | source)
XLA Modules:
  0.0 662.8 jit_solution(13295500259745819986)
XLA Ops:
  10.9 56.7 %all-gather.2.cloned.1.call-done = bf16[8,64,2,3584]{3,2,0,1:T(2,128)(2,1)} async-done(((bf16[1,64,2,3584]{3,2,0,1:T(2,128)(2,1)}), bf16[8,64,2,3584]{3,2,0,1:T(2,128)(2,1)}) %all-gather.2.cloned.1.call-update) | async-done | bytes 7340048 | tf_op jit(solution)/shard_map/all_gather | solution.py:52
  67.6 1.6 constant_dynamic-update-slice_fusion.63
  70.8 1.6 constant_dynamic-update-slice_fusion.61
  75.7 1.6 constant_dynamic-update-slice_fusion.58
  77.3 1.6 constant_dynamic-update-slice_fusion.57
  80.6 1.6 constant_dynamic-update-slice_fusion.55
  82.2 1.7 constant_dynamic-update-slice_fusion.54
  85.5 1.6 constant_dynamic-update-slice_fusion.52
  87.1 1.6 constant_dynamic-update-slice_fusion.51
  90.3 1.6 constant_dynamic-update-slice_fusion.49
  91.9 1.6 constant_dynamic-update-slice_fusion.48
  93.6 1.6 constant_dynamic-update-slice_fusion.47
  95.2 1.6 constant_dynamic-update-slice_fusion.46
  100.1 1.6 constant_dynamic-update-slice_fusion.43
  101.7 1.6 constant_dynamic-update-slice_fusion.42
  103.3 1.6 constant_dynamic-update-slice_fusion.41
  108.2 1.6 constant_dynamic-update-slice_fusion.38
  111.4 1.6 constant_dynamic-update-slice_fusion.36
  113.0 1.6 constant_dynamic-update-slice_fusion.35
  114.7 1.6 constant_dynamic-update-slice_fusion.34
  116.3 1.6 constant_dynamic-update-slice_fusion.33
  117.9 1.6 constant_dynamic-update-slice_fusion.32
  119.5 1.6 constant_dynamic-update-slice_fusion.31
  121.2 1.6 constant_dynamic-update-slice_fusion.30
  124.4 1.6 constant_dynamic-update-slice_fusion.28
  126.0 1.6 constant_dynamic-update-slice_fusion.27
  129.3 1.6 constant_dynamic-update-slice_fusion.25
  134.1 1.6 constant_dynamic-update-slice_fusion.22
  135.7 1.6 constant_dynamic-update-slice_fusion.21
  137.4 1.6 constant_dynamic-update-slice_fusion.20
  139.0 1.6 constant_dynamic-update-slice_fusion.19
  140.6 1.6 constant_dynamic-update-slice_fusion.18
  142.3 1.6 constant_dynamic-update-slice_fusion.17
  147.1 1.6 constant_dynamic-update-slice_fusion.14
  148.8 1.6 constant_dynamic-update-slice_fusion.13
  150.4 1.6 constant_dynamic-update-slice_fusion.12
  152.0 1.6 constant_dynamic-update-slice_fusion.11
  153.6 1.6 constant_dynamic-update-slice_fusion.10
  155.3 1.6 constant_dynamic-update-slice_fusion.9
  156.9 1.6 constant_dynamic-update-slice_fusion.8
  158.5 1.6 constant_dynamic-update-slice_fusion.7
  160.1 1.6 constant_dynamic-update-slice_fusion.6
  163.4 1.6 constant_dynamic-update-slice_fusion.4
  165.0 1.6 constant_dynamic-update-slice_fusion.3
  166.6 1.6 constant_dynamic-update-slice_fusion.2
  168.2 1.6 constant_dynamic-update-slice_fusion.1
  171.5 16.2 %all-to-all-start = ((bf16[64,8,1,2,3584]{4,3,1,2,0:T(2,128)(2,1)}), bf16[64,8,1,2,3584]{4,3,1,2,0:T(2,128)(2,1)}, u32[]{:S(2)}, u32[]{:S(2)}) async-start(bf16[64,8,1,2,3584]{4,3,1,2,0:T(2,128)(2,1)} %constant_dynamic-update-slice_fusion), calls=%async_computation | async-start | bytes 14680064 | tf_op jit(solution)/shard_map/all_to_all | solution.py:56
  187.9 323.7 %all-to-all-done = bf16[64,8,1,2,3584]{4,3,1,2,0:T(2,128)(2,1)} async-done(((bf16[64,8,1,2,3584]{4,3,1,2,0:T(2,128)(2,1)}), bf16[64,8,1,2,3584]{4,3,1,2,0:T(2,128)(2,1)}, u32[]{:S(2)}, u32[]{:S(2)}) %all-to-all-start) | async-done | bytes 7340064 | tf_op jit(solution)/shard_map/all_to_all | solution.py:56
  511.5 7.1 %copy.197 = bf16[64,8,1,2,3584]{4,0,3,2,1:T(8,128)(2,1)S(1)} copy(bf16[64,8,1,2,3584]{4,3,1,2,0:T(2,128)(2,1)} %all-to-all-done) | data formatting | bytes 14680064 | tf_op jit(solution)/shard_map/all_to_all | solution.py:56
  518.6 7.1 %copy.180 = bf16[8,64,1,2,3584]{4,3,1,0,2:T(2,128)(2,1)} copy(bf16[8,64,1,2,3584]{4,1,3,2,0:T(8,128)(2,1)S(1)} %bitcast.307) | data formatting | bytes 14680064 | tf_op jit(solution)/shard_map/reshape | solution.py:55
  525.7 15.5 %reshape_reshape.3 = bf16[1024,3584]{1,0:T(8,128)(2,1)} reshape(bf16[8,64,1,2,3584]{4,3,1,0,2:T(2,128)(2,1)} %copy.180) | data formatting | bytes 14680064 | tf_op jit(solution)/shard_map/reshape;reshape | solution.py:65
  541.2 5.6 multiply_reduce_fusion
  546.8 10.4 %psum.7 = f32[8,128]{1,0:T(8,128)S(1)} all-reduce(f32[8,128]{1,0:T(8,128)S(1)} %bitcast.309), channel_id=1, replica_groups=mesh['node'=64,'local'=8] {'local'}, use_global_device_ids=true, to_apply=%region_5.6 | all-reduce | flops 1024 | bytes 8192 | tf_op jit(solution)/shard_map/psum | solution.py:85
  558.0 7.0 %all-to-all-start.1 = ((f32[64,1,2]{2,1,0:T(1,128)}), f32[64,1,2]{2,1,0:T(1,128)}, u32[]{:S(2)}, u32[]{:S(2)}) async-start(f32[64,1,2]{2,1,0:T(1,128)} %bitcast.69), calls=%async_computation.1 | async-start | bytes 65536 | tf_op jit(solution)/shard_map/all_to_all | solution.py:87
  566.9 12.1 %all-to-all-done.1 = f32[64,1,2]{2,1,0:T(1,128)} async-done(((f32[64,1,2]{2,1,0:T(1,128)}), f32[64,1,2]{2,1,0:T(1,128)}, u32[]{:S(2)}, u32[]{:S(2)}) %all-to-all-start.1) | async-done | bytes 544 | tf_op jit(solution)/shard_map/all_to_all | solution.py:87
  581.5 11.1 %all_gather.7 = bf16[8,64,2]{1,2,0:T(2,128)(2,1)S(1)} all-gather(bf16[1,64,2]{1,2,0:T(2,128)(2,1)S(1)} %copy.184), channel_id=1, replica_groups=mesh['node'=64,'local'=8] {'local'}, dimensions={0}, use_global_device_ids=true | all-gather | bytes 2304 | tf_op jit(solution)/shard_map/all_gather | solution.py:53
  593.4 4.8 all-to-all-start.2
  598.8 13.6 %all-to-all-done.2 = bf16[8,64,2]{0,2,1:T(2,128)(2,1)S(1)} async-done(((bf16[8,64,2]{0,2,1:T(2,128)(2,1)}), bf16[8,64,2]{0,2,1:T(2,128)(2,1)S(1)}, u32[]{:S(2)}, u32[]{:S(2)}) %all-to-all-start.2) | async-done | bytes 2080 | tf_op jit(solution)/shard_map/all_to_all | solution.py:63
  612.6 7.8 %multiply_convert_fusion = bf16[8,64,1,2,3584]{4,1,3,2,0:T(8,128)(2,1)S(1)} fusion(f32[8,64,2]{1,2,0:T(2,128)S(1)} %copy.188, bf16[64,8,1,2,3584]{4,3,1,2,0:T(2,128)(2,1)} %all-to-all-done), kind=kLoop, calls=%fused_computation | loop fusion | flops 11010048 | bytes 14684160 | tf_op jit(solution)/shard_map/convert_element_type | solution.py:74
  620.4 7.1 %copy.189 = bf16[8,64,1,2,3584]{4,3,1,0,2:T(2,128)(2,1)} copy(bf16[8,64,1,2,3584]{4,1,3,2,0:T(8,128)(2,1)S(1)} %multiply_convert_fusion) | data formatting | bytes 14680064 | tf_op jit(solution)/shard_map/convert_element_type | solution.py:74
  627.4 15.4 %convert_element_type.90 = bf16[1024,3584]{1,0:T(8,128)(2,1)} reshape(bf16[8,64,1,2,3584]{4,3,1,0,2:T(2,128)(2,1)} %copy.189) | data formatting | bytes 14680064 | tf_op jit(solution)/shard_map/convert_element_type | solution.py:74
  642.9 7.6 %fusion.5 = (bf16[1,128,3584]{1,2,0:T(8,128)(2,1)}, bf16[1,128,3584]{1,2,0:T(8,128)(2,1)}) fusion(bf16[1,128,3584]{1,2,0:T(8,128)(2,1)} %copy.190, bf16[1,128,3584]{1,2,0:T(8,128)(2,1)S(1)} %copy.181, bf16[1024,3584]{1,0:T(8,128)(2,1)} %convert_element_type.90, bf16[1,1024,128]{2,1,0:T(8,128)(2,1)S(1)} %copy-done.4), kind=kOutput, calls=%fused_computation.12 | convolution fusion | flops 946405376 | bytes 11272192 | tf_op jit(solution)/shard_map/dot_general | solution.py:75
  650.5 2.2 copy.192
  652.7 2.2 copy.193
  (62 shorter events, 42.3 us)
Async XLA Ops:
  7.2 2.0 copy-start
  7.2 60.4 %all-gather.2.cloned.1.call-start = ((), (), s32[]{:S(2)}) async-start(), calls=%async_computation.3 | async-start | bytes 8257536 | tf_op jit(solution)/shard_map/all_gather | solution.py:52
  171.5 16.2 %copy-start.4 = (bf16[1,1024,128]{2,1,0:T(8,128)(2,1)S(1)}, bf16[1,1024,128]{2,1,0:T(8,128)(2,1)}, u32[]{:S(2)}) copy-start(bf16[1,1024,128]{2,1,0:T(8,128)(2,1)} %param.9) | copy-start | bytes 786436
  171.5 340.0 %all-to-all-start = ((bf16[64,8,1,2,3584]{4,3,1,2,0:T(2,128)(2,1)}), bf16[64,8,1,2,3584]{4,3,1,2,0:T(2,128)(2,1)}, u32[]{:S(2)}, u32[]{:S(2)}) async-start(bf16[64,8,1,2,3584]{4,3,1,2,0:T(2,128)(2,1)} %constant_dynamic-update-slice_fusion), calls=%async_computation | async-start | bytes 14680064 | tf_op jit(solution)/shard_map/all_to_all | solution.py:56
  525.7 15.5 %copy-start.2 = (bf16[1,128,3584]{2,1,0:T(8,128)(2,1)S(1)}, bf16[1,128,3584]{2,1,0:T(8,128)(2,1)}, u32[]{:S(2)}) copy-start(bf16[1,128,3584]{2,1,0:T(8,128)(2,1)} %param.10) | copy-start | bytes 2752516
  541.2 23.8 %copy-start.5 = (f32[128,8]{0,1:T(8,128)S(1)}, f32[128,8]{0,1:T(8,128)}, u32[]{:S(2)}) copy-start(f32[128,8]{0,1:T(8,128)} %param.8) | copy-start | bytes 12292
  541.2 24.4 %copy-start.3 = (bf16[1,128,3584]{2,1,0:T(8,128)(2,1)S(1)}, bf16[1,128,3584]{2,1,0:T(8,128)(2,1)}, u32[]{:S(2)}) copy-start(bf16[1,128,3584]{2,1,0:T(8,128)(2,1)} %param.11) | copy-start | bytes 2752516
  558.0 21.0 %all-to-all-start.1 = ((f32[64,1,2]{2,1,0:T(1,128)}), f32[64,1,2]{2,1,0:T(1,128)}, u32[]{:S(2)}, u32[]{:S(2)}) async-start(f32[64,1,2]{2,1,0:T(1,128)} %bitcast.69), calls=%async_computation.1 | async-start | bytes 65536 | tf_op jit(solution)/shard_map/all_to_all | solution.py:87
  593.4 19.0 %all-to-all-start.2 = ((bf16[8,64,2]{0,2,1:T(2,128)(2,1)}), bf16[8,64,2]{0,2,1:T(2,128)(2,1)S(1)}, u32[]{:S(2)}, u32[]{:S(2)}) async-start(bf16[8,64,2]{0,2,1:T(2,128)(2,1)} %copy.185), calls=%async_computation.2 | async-start | bytes 65536 | tf_op jit(solution)/shard_map/all_to_all | solution.py:63
  642.9 13.1 %copy-start.1 = (bf16[128,3584]{1,0:T(8,128)(2,1)S(1)}, bf16[128,3584]{1,0:T(8,128)(2,1)}, u32[]{:S(2)}) copy-start(bf16[128,3584]{1,0:T(8,128)(2,1)} %param.6) | copy-start | bytes 2752516
Sparse Core Ops, SparseCore 0:
  11.0 56.5 all-gather.1
